TPU v7x, 32 devices: a whole 2x2x4 slice. The times are simulated.
32 devices in a mesh: ctx: 8 (over y, x, core), head: 4 (over z).
Axes of the slice: x: 2, y: 2, z: 4, core: 2. Of those that a mesh axis runs over, the one named last changes fastest.
Arguments:
- inputs: bfloat16 [2048, 4096], P('ctx', 'head'), may hold values from -6 to 6
- log_decay: float32 [64, 2048], P('head', 'ctx'), may hold values from -1 to 0
- in_b: bfloat16 [2048, 512], P('ctx', 'head'), may hold values from -0.20996094 to 0.20996094
- in_c: bfloat16 [2048, 512], P('ctx', 'head'), may hold values from -0.20996094 to 0.20996094
- seg_ids: int32 [2048], P('ctx'), may hold values from 0 to 5, never falling along the last dimension, each value on 1 to 1024 neighbouring positions
- skip_gain: float32 [64], P('head'), may hold values from 0.1 to 1.9
- grad_out: bfloat16 [2048, 4096], P('ctx', 'head'), may hold values from -0.119628906 to 0.119628906
Outputs:
- ssd_out: bfloat16 [2048, 4096], P('ctx', 'head')
- grad_x: bfloat16 [2048, 4096], P('ctx', 'head')
- grad_b: bfloat16 [2048, 512], P('ctx', 'head')
- grad_c: bfloat16 [2048, 512], P('ctx', 'head')
All inputs are finite; a program needn't handle non-finite values.
Results may differ from a plain program's by a relative error of at most 0.0017.
Values may be sent and summed in bfloat16 or wider, within the bound.
A program may use at most 192 MiB of HBM per device.

v0:
```python
import jax
import jax.numpy as jnp
from jax import lax
from jax.sharding import PartitionSpec as P

BLOCK = 256


precise = lax.Precision.HIGH


def from_partner(array, axis, distance):
    return lax.ppermute(array, axis, [(i, i ^ 1 << distance) for i in range(lax.axis_size(axis))])


def carried_in(array, axis, combine, identity, reverse):
    peers, position = (lax.axis_size(axis), lax.axis_index(axis))
    everything = jax.tree.map(lambda part: lax.all_gather(part, axis), array)
    start = jax.tree.map(
        lambda part, zero: jnp.broadcast_to(jnp.asarray(zero, part.dtype), part.shape),
        array,
        identity,
    )

    def hop(k, before):
        at = peers - 1 - k if reverse else k
        reached = at > position if reverse else at < position
        new = combine(before, jax.tree.map(lambda part: part[at], everything))
        return jax.tree.map(lambda a, b: jnp.where(reached, a, b), new, before)

    return lax.fori_loop(0, peers, hop, start)


def matches(left_seg, right_seg):
    return jnp.where((left_seg < 0) | (right_seg < 0) | (left_seg == right_seg), 1.0, 0.0).astype(
        jnp.float32
    )


def forward_combine(earlier, later):
    early_keep, early_state, early_first, early_last = earlier
    later_keep, later_state, later_first, later_last = later
    passing = later_keep * matches(early_last, later_first)
    return (
        early_keep * passing,
        passing[:, None, None] * early_state + later_state,
        jnp.where(early_first < 0, later_first, early_first),
        jnp.where(later_last < 0, early_last, later_last),
    )


def backward_combine(earlier, later):
    early_keep, early_state, early_first, early_last = earlier
    later_keep, later_state, later_first, later_last = later
    passing = later_keep * matches(later_last, early_first)
    return (
        early_keep * passing,
        passing[:, None, None] * early_state + later_state,
        jnp.where(later_first < 0, early_first, later_first),
        jnp.where(early_last < 0, later_last, early_last),
    )


def block_tables(decay_rows, seg_block, prev_seg):
    cum_decay = jnp.cumsum(decay_rows, axis=1)
    total_decay = cum_decay[:, -1]
    last_seg = seg_block[-1]
    row_index = jnp.arange(seg_block.shape[0])
    keep_mask = (row_index[:, None] >= row_index[None, :]) & (
        seg_block[:, None] == seg_block[None, :]
    )
    decay_table = jnp.exp(
        jnp.where(keep_mask[None], cum_decay[:, :, None] - cum_decay[:, None, :], -jnp.inf)
    )
    start_weight = jnp.exp(cum_decay) * (seg_block == prev_seg).astype(jnp.float32)[None]
    end_weight = (
        jnp.exp(total_decay[:, None] - cum_decay)
        * (seg_block == last_seg).astype(jnp.float32)[None]
    )
    carry_gain = jnp.exp(total_decay) * (last_seg == prev_seg).astype(jnp.float32)
    return (decay_table, start_weight, end_weight, carry_gain, last_seg)


def local_pass(
    input_heads,
    grad_heads,
    log_decay,
    seg_float,
    full_b,
    full_c,
    state_start,
    prev_start,
    adjoint_start,
):
    token_count = input_heads.shape[0]
    block_count = token_count // BLOCK
    state_now = state_start
    block_index = 0
    x_block = input_heads
    b_block = full_b
    c_block = full_c
    decay_table, start_weight, end_weight, carry_gain, last_seg = block_tables(
        log_decay, seg_float, prev_start
    )
    score = lax.dot_general(
        c_block, b_block, (((1,), (1,)), ((), ())), preferred_element_type=jnp.float32
    )
    mixed = (decay_table * score[None]).astype(jnp.bfloat16)
    inner_term = jnp.einsum("hij,jhp->ihp", mixed, x_block, preferred_element_type=jnp.float32)
    outer_term = (
        jnp.einsum(
            "in,hpn->ihp", c_block, state_now, precision=precise, preferred_element_type=jnp.float32
        )
        * start_weight.T[:, :, None]
    )
    weighted = x_block.astype(jnp.float32) * end_weight.T[:, :, None]
    fresh_state = jnp.einsum(
        "jhp,jn->hpn", weighted, b_block, precision=precise, preferred_element_type=jnp.float32
    )
    tables = [(prev_start, mixed, start_weight, end_weight, carry_gain, state_now, weighted)]
    forward_terms = inner_term + outer_term
    state_now = carry_gain[:, None, None] * state_now + fresh_state
    adjoint = adjoint_start
    grad_terms = [None] * block_count
    bmap_terms = [None] * block_count
    cmap_terms = [None] * block_count
    for block_index in reversed(range(block_count)):
        x_block = input_heads
        b_block = full_b
        c_block = full_c
        block_prev, mixed, start_weight, end_weight, carry_gain, state_now, weighted = tables[
            block_index
        ]
        decay_table = block_tables(log_decay, seg_float, block_prev)[0]
        grad_inputs = jnp.einsum(
            "hij,ihp->jhp", mixed, grad_heads, preferred_element_type=jnp.float32
        )
        grad_inputs = (
            grad_inputs
            + jnp.einsum(
                "jn,hpn->jhp",
                b_block,
                adjoint,
                precision=precise,
                preferred_element_type=jnp.float32,
            )
            * end_weight.T[:, :, None]
        )
        grad_mix = jnp.einsum(
            "ihp,jhp->hij", grad_heads, x_block, preferred_element_type=jnp.float32
        )
        dscore = jnp.sum(grad_mix * decay_table, axis=0)
        grad_bmap = lax.dot_general(
            dscore,
            c_block,
            (((0,), (0,)), ((), ())),
            precision=precise,
            preferred_element_type=jnp.float32,
        )
        grad_bmap = grad_bmap + jnp.einsum("jhp,hpn->jn", weighted, adjoint, precision=precise)
        grad_start = grad_heads.astype(jnp.float32) * start_weight.T[:, :, None]
        grad_cmap = jnp.dot(dscore, b_block, precision=precise, preferred_element_type=jnp.float32)
        grad_cmap = grad_cmap + jnp.einsum("ihp,hpn->in", grad_start, state_now, precision=precise)
        back_state = jnp.einsum(
            "ihp,in->hpn",
            grad_start,
            c_block,
            precision=precise,
            preferred_element_type=jnp.float32,
        )
        adjoint = back_state + carry_gain[:, None, None] * adjoint
        grad_terms[block_index] = grad_inputs
        bmap_terms[block_index] = grad_bmap
        cmap_terms[block_index] = grad_cmap
    return (forward_terms, grad_terms[0], bmap_terms[0], cmap_terms[0])


def per_device(inputs, log_decay, in_b, in_c, seg_ids, skip_gain, grad_out):
    token_count, feature_width = inputs.shape
    head_count = log_decay.shape[0]
    head_width = feature_width // head_count
    half_cols = in_b.shape[1]
    state_width = 2 * half_cols
    pair_side = lax.axis_index("head") % 2
    is_lower = pair_side == 0
    other_b, other_c = from_partner((in_b, in_c), "head", 0)
    full_b = jnp.concatenate(
        [jnp.where(is_lower, in_b, other_b), jnp.where(is_lower, other_b, in_b)], axis=1
    )
    full_c = jnp.concatenate(
        [jnp.where(is_lower, in_c, other_c), jnp.where(is_lower, other_c, in_c)], axis=1
    )
    input_heads = inputs.reshape(token_count, head_count, head_width)
    grad_heads = grad_out.reshape(token_count, head_count, head_width)
    input_float = input_heads.astype(jnp.float32)
    grad_float = grad_heads.astype(jnp.float32)
    seg_float = seg_ids.astype(jnp.float32)
    first_seg = seg_float[0]
    last_seg = seg_float[-1]
    cum_device = jnp.cumsum(log_decay, axis=1)
    total_device = cum_device[:, -1]
    keep_device = jnp.exp(total_device) * (first_seg == last_seg).astype(jnp.float32)
    end_device = (
        jnp.exp(total_device[:, None] - cum_device)
        * (seg_float == last_seg).astype(jnp.float32)[None]
    )
    head_device = jnp.exp(cum_device) * (seg_float == first_seg).astype(jnp.float32)[None]
    weighted_inputs = input_float * end_device.T[:, :, None]
    fresh_device = jnp.einsum(
        "jhp,jn->hpn",
        weighted_inputs,
        full_b,
        precision=precise,
        preferred_element_type=jnp.float32,
    )
    back_device = jnp.einsum(
        "ihp,in->hpn",
        grad_float * head_device.T[:, :, None],
        full_c,
        precision=precise,
        preferred_element_type=jnp.float32,
    )
    identity = (
        jnp.ones((head_count,), jnp.float32),
        jnp.zeros((head_count, head_width, state_width), jnp.float32),
        jnp.full((), -1.0, jnp.float32),
        jnp.full((), -1.0, jnp.float32),
    )
    incoming = carried_in(
        (keep_device, fresh_device, first_seg, last_seg), "ctx", forward_combine, identity, False
    )
    outgoing = carried_in(
        (keep_device, back_device, first_seg, last_seg), "ctx", backward_combine, identity, True
    )
    state_in = incoming[1]
    prev_last = incoming[3]
    adjoint_end = outgoing[1] * matches(last_seg, outgoing[2])
    ssd_terms, grad_terms, grad_bmap, grad_cmap = local_pass(
        input_heads,
        grad_heads,
        log_decay,
        seg_float,
        full_b,
        full_c,
        state_in,
        prev_last,
        adjoint_end,
    )
    own_start = pair_side * half_cols
    other_bmap, other_cmap = from_partner((grad_bmap, grad_cmap), "head", 0)
    bmap_mine = lax.dynamic_slice_in_dim(grad_bmap + other_bmap, own_start, half_cols, 1)
    cmap_mine = lax.dynamic_slice_in_dim(grad_cmap + other_cmap, own_start, half_cols, 1)
    gains = skip_gain[None, :, None]
    ssd_out = (
        (ssd_terms + gains * input_float).astype(jnp.bfloat16).reshape(token_count, feature_width)
    )
    grad_x = (
        (grad_terms + gains * grad_float).astype(jnp.bfloat16).reshape(token_count, feature_width)
    )
    return (ssd_out, grad_x, bmap_mine.astype(jnp.bfloat16), cmap_mine.astype(jnp.bfloat16))


def solution(mesh):
    return jax.shard_map(
        per_device,
        mesh=mesh,
        in_specs=(
            P("ctx", "head"),
            P("head", "ctx"),
            P("ctx", "head"),
            P("ctx", "head"),
            P("ctx"),
            P("head"),
            P("ctx", "head"),
        ),
        out_specs=(P("ctx", "head"), P("ctx", "head"), P("ctx", "head"), P("ctx", "head")),
        check_vma=False,
    )
```

profile of v0, /device:TPU:0, one launch (start us, length us, event | category | flops | bytes accessed | tf_op | source)
XLA Modules:
  0.0 196.4 jit_solution(9668245796450096215)
XLA Ops:
  7.2 3.1 %collective-permute-start.1 = (bf16[256,128]{1,0:T(8,128)(2,1)}, bf16[256,128]{1,0:T(8,128)(2,1)S(1)}, u32[]{:S(2)}, u32[]{:S(2)}) collective-permute-start(bf16[256,128]{1,0:T(8,128)(2,1)} %param.13), channel_id=1, source_target_pairs={{0,1},{1,0},{2,3},{3,2},{4,5},{5,4},{6,7},{7,6},{8,9},{9,8},{10,11... | collective-permute-start | bytes 196616 | tf_op jit(solution)/shard_map/ppermute | solution.py:13
  14.8 1.9 compare_convert_fusion
  21.8 4.0 %collective-permute-done = bf16[256,128]{1,0:T(8,128)(2,1)S(1)} collective-permute-done((bf16[256,128]{1,0:T(8,128)(2,1)S(1)}, bf16[256,128]{1,0:T(8,128)(2,1)S(1)}, u32[]{:S(2)}, u32[]{:S(2)}) %collective-permute-start) | collective-permute-done | bytes 65568 | tf_op jit(solution)/shard_map/ppermute | solution.py:13
  29.0 12.6 %all-reduce.3 = (f32[128]{0:T(128)S(1)}, f32[8]{0:T(128)S(1)}, f32[8]{0:T(128)S(1)}) all-reduce(f32[128]{0:T(128)S(1)} %dynamic-update-slice, f32[8]{0:T(128)S(1)} %slice_dynamic-update-slice_fusion.1, f32[8]{0:T(128)S(1)} %get-tuple-element.462), channel_id=2, replica_groups=mesh['ctx'=8,'head'=4] {'ctx'}, use_global_device_ids=true, to_apply=%add | all-reduce | flops 144 | bytes 1152
  42.4 2.2 %multiply_reduce_fusion = f32[256,256]{1,0:T(8,128)} fusion(bf16[256,16,64]{0,2,1:T(8,128)(2,1)S(1)} %bitcast.98, bf16[256,16,64]{0,2,1:T(8,128)(2,1)S(1)} %bitcast.93, f32[16,256]{1,0:T(8,128)S(1)} %copy_bitcast_fusion, pred[256,256]{1,0:T(8,128)(4,1)S(1)} %fusion.34), kind=kOutput, calls=%fused_computation.6 | convolution fusion | flops 138346496 | bytes 1392640 | tf_op jit(solution)/shard_map/ihp,jhp->hij/dot_general | solution.py:149
  44.8 2.1 %fusion.15 = f32[256,16,64]{0,2,1:T(8,128)} fusion(bf16[256,16,64]{0,2,1:T(8,128)(2,1)S(1)} %bitcast.99, f32[256,256]{1,0:T(8,128)S(1)} %fusion.43, f32[16,256]{1,0:T(8,128)S(1)} %copy_bitcast_fusion, pred[256,256]{1,0:T(8,128)(4,1)S(1)} %fusion.34), kind=kOutput, calls=%fused_computation.25 | convolution fusion | flops 138412032 | bytes 1916928 | tf_op jit(solution)/shard_map/hij,ihp->jhp/dot_general | solution.py:135
  46.9 2.2 %fusion.14 = f32[256,16,64]{0,2,1:T(8,128)} fusion(bf16[256,16,64]{0,2,1:T(8,128)(2,1)S(1)} %bitcast.94, f32[256,256]{1,0:T(8,128)S(1)} %fusion.43, f32[16,256]{1,0:T(8,128)S(1)} %copy_bitcast_fusion, pred[256,256]{1,0:T(8,128)(4,1)S(1)} %fusion.34), kind=kOutput, calls=%fused_computation.24 | convolution fusion | flops 138412032 | bytes 1916928 | tf_op jit(solution)/shard_map/hij,jhp->ihp/dot_general | solution.py:109
  49.1 27.2 %all-gather.6.cloned.1.call-done = f32[128,64,256]{2,1,0:T(8,128)} async-done(((f32[16,64,256]{2,1,0:T(8,128)}), f32[128,64,256]{2,1,0:T(8,128)}) %all-gather.6.cloned.1.call-update) | async-done | bytes 8388624 | tf_op jit(solution)/shard_map/all_gather | solution.py:18
  76.3 38.7 %while.34 = (s32[]{:T(128)}, f32[16,64,256]{2,1,0:T(8,128)S(1)}, f32[]{:T(128)}, s32[]{:T(128)}, f32[8,16]{1,0:T(8,128)S(1)}, /*index=5*/f32[8]{0:T(128)S(1)}, f...) while((s32[]{:T(128)}, f32[16,64,256]{2,1,0:T(8,128)S(1)}, ...), condition=%wide.region_3.4_spmd.clone, body=%wide.region_2.3_spmd.clone.sunk | while | flops 1048605 | bytes 3146174 | solution.py:31
  78.0 1.5 fusion.55
  82.9 1.5 fusion.55
  87.7 1.5 fusion.55
  92.5 1.5 fusion.55
  97.4 1.5 fusion.55
  116.1 1.9 convolution_add_fusion
  118.0 1.6 collective-permute-start.3
  119.7 13.0 %all-gather.8.cloned.1.call-done = f32[128,64,256]{2,1,0:T(8,128)} async-done(((f32[16,64,256]{2,1,0:T(8,128)}), f32[128,64,256]{2,1,0:T(8,128)}) %all-gather.8.cloned.1.call-update) | async-done | bytes 8388624 | tf_op jit(solution)/shard_map/all_gather | solution.py:18
  132.7 42.4 %while.35 = (s32[]{:T(128)}, f32[16,64,256]{2,1,0:T(8,128)S(1)}, f32[]{:T(128)}, s32[]{:T(128)}, f32[8,16]{1,0:T(8,128)S(1)}, /*index=5*/f32[8]{0:T(128)S(1)}, f...) while((s32[]{:T(128)}, f32[16,64,256]{2,1,0:T(8,128)S(1)}, ...), condition=%wide.region_5.6_spmd.clone, body=%wide.region_4.5_spmd.clone.sunk | while | flops 1048609 | bytes 3146236 | solution.py:31
  134.6 1.5 fusion.56
  139.9 1.5 fusion.56
  145.2 1.5 fusion.56
  150.6 1.5 fusion.56
  155.9 1.5 fusion.56
  161.2 1.5 fusion.56
  166.5 1.5 fusion.56
  171.8 1.5 fusion.56
  176.7 2.0 %convolution_add_fusion.1 = f32[256,256]{1,0:T(8,128)} fusion(f32[256,256]{1,0:T(8,128)S(1)} %fusion.24, f32[256,256]{1,0:T(8,128)} %multiply_reduce_fusion, bf16[256,128]{1,0:T(8,128)(2,1)S(1)} %get-tuple-element.455, bf16[256,128]{1,0:T(8,128)(2,1)S(1)} %get-tuple-element.454), kind=kOutput, calls=%fused_computation.40 | convolution fusion | flops 100990976 | bytes 917504 | tf_op jit(solution)/shard_map/dot_general | solution.py:153
  178.7 1.5 collective-permute-start.2
  180.2 2.6 %fusion.20 = bf16[256,16,64]{0,2,1:T(8,128)(2,1)} fusion(f32[256,16,64]{0,2,1:T(8,128)} %fusion.15, bf16[256,16,64]{0,2,1:T(8,128)(2,1)S(1)} %bitcast.101, f32[16,64,256]{2,1,0:T(8,128)S(1)} %get-tuple-element.345, f32[]{:T(128)S(6)} %select_n.157, f32[16]{0:T(128)S(1)} %copy-done.5, f32[256,16]{0,1:T(8,128)S(1)} %get-tuple-element.459, ...), kind=kOutput, calls=%fused_computation.34 | convolution fusion | flops 404750336 | bytes 3293252 | tf_op jit(solution)/shard_map/jn,hpn->jhp/dot_general | solution.py:140
  183.3 2.0 %copy.38 = bf16[256,1024]{1,0:T(8,128)(2,1)} copy(bf16[256,1024]{0,1:T(8,128)(2,1)} %bitcast.104) | data formatting | bytes 1048576
  186.4 1.6 fusion.35
  188.0 1.6 fusion.36
  (104 shorter events, 37.8 us)
Async XLA Ops:
  7.2 9.5 %copy-start = (f32[16,256]{1,0:T(8,128)S(1)}, f32[16,256]{1,0:T(8,128)}, u32[]{:S(2)}) copy-start(f32[16,256]{1,0:T(8,128)} %param.12) | copy-start | bytes 49156
  7.2 14.3 %copy-start.3 = (bf16[256,128]{1,0:T(8,128)(2,1)S(1)}, bf16[256,128]{1,0:T(8,128)(2,1)}, u32[]{:S(2)}) copy-start(bf16[256,128]{1,0:T(8,128)(2,1)} %param.14) | copy-start | bytes 196612
  7.2 14.4 %copy-start.2 = (bf16[256,1024]{1,0:T(8,128)(2,1)S(1)}, bf16[256,1024]{1,0:T(8,128)(2,1)}, u32[]{:S(2)}) copy-start(bf16[256,1024]{1,0:T(8,128)(2,1)} %param.17) | copy-start | bytes 1572868
  7.2 69.1 %all-gather.6.cloned.1.call-start = ((), (), s32[]{:S(2)}) async-start(), calls=%async_computation | async-start | bytes 9437184 | tf_op jit(solution)/shard_map/all_gather | solution.py:18
  7.2 11.9 %collective-permute-start.1 = (bf16[256,128]{1,0:T(8,128)(2,1)}, bf16[256,128]{1,0:T(8,128)(2,1)S(1)}, u32[]{:S(2)}, u32[]{:S(2)}) collective-permute-start(bf16[256,128]{1,0:T(8,128)(2,1)} %param.13), channel_id=1, source_target_pairs={{0,1},{1,0},{2,3},{3,2},{4,5},{5,4},{6,7},{7,6},{8,9},{9,8},{10,11... | collective-permute-start | bytes 196616 | tf_op jit(solution)/shard_map/ppermute | solution.py:13
  21.4 111.3 %all-gather.8.cloned.1.call-start = ((), (), s32[]{:S(2)}) async-start(), calls=%async_computation.1 | async-start | bytes 9437184 | tf_op jit(solution)/shard_map/all_gather | solution.py:18
  21.5 4.3 %collective-permute-start = (bf16[256,128]{1,0:T(8,128)(2,1)S(1)}, bf16[256,128]{1,0:T(8,128)(2,1)S(1)}, u32[]{:S(2)}, u32[]{:S(2)}) collective-permute-start(bf16[256,128]{1,0:T(8,128)(2,1)S(1)} %copy-done.3), channel_id=1, source_target_pairs={{0,1},{1,0},{2,3},{3,2},{4,5},{5,4},{6,7},{7,6},{8,9},{9,8},{10,11... | collective-permute-start | bytes 196616 | tf_op jit(solution)/shard_map/ppermute | solution.py:13
  76.3 38.7 %copy-start.4 = (s32[256]{0:T(256)S(1)}, s32[256]{0:T(256)}, u32[]{:S(2)}) copy-start(s32[256]{0:T(256)} %param.15) | copy-start | bytes 3076
  118.0 68.3 %collective-permute-start.3 = (f32[256,256]{1,0:T(8,128)}, f32[256,256]{1,0:T(8,128)}, u32[]{:S(2)}, u32[]{:S(2)}) collective-permute-start(f32[256,256]{1,0:T(8,128)} %convolution_add_fusion), channel_id=1, source_target_pairs={{0,1},{1,0},{2,3},{3,2},{4,5},{5,4},{6,7},{7,6},{8,9},{9,8},{10,11... | collective-permute-start | bytes 786440 | tf_op jit(solution)/shard_map/ppermute | solution.py:13
  132.7 47.5 %copy-start.5 = (f32[16]{0:T(128)S(1)}, f32[16]{0:T(128)}, u32[]{:S(2)}) copy-start(f32[16]{0:T(128)} %param.16) | copy-start | bytes 196
  175.7 7.1 %copy-start.1 = (f32[256,16,64]{0,2,1:T(8,128)S(1)}, f32[256,16,64]{0,2,1:T(8,128)}, u32[]{:S(2)}) copy-start(f32[256,16,64]{0,2,1:T(8,128)} %fusion.14) | copy-start | bytes 3145732
  178.7 9.3 %collective-permute-start.2 = (f32[256,256]{1,0:T(8,128)}, f32[256,256]{1,0:T(8,128)}, u32[]{:S(2)}, u32[]{:S(2)}) collective-permute-start(f32[256,256]{1,0:T(8,128)} %convolution_add_fusion.1), channel_id=1, source_target_pairs={{0,1},{1,0},{2,3},{3,2},{4,5},{5,4},{6,7},{7,6},{8,9},{9,8},{10,11... | collective-permute-start | bytes 786440 | tf_op jit(solution)/shard_map/ppermute | solution.py:13
Sparse Core Ops, SparseCore 0:
  21.6 54.7 all-gather.5
  78.2 54.4 all-gather.7
where the time goes:
time: 198 us; the launch traced here: 196 us
  waiting for transfers between devices  44.3 us (22%)
  loops' own time  39.2 us (20%)
  other arithmetic  31.4 us (16%)
  local copies, waits for them, and re-layouts  26.6 us (13%)
  matrix products  18.6 us (9%)
  between operations  17.3 us (9%)
  blocking collectives  12.6 us (6%)
  starting transfers between devices  6.41 us (3%)
    all_gather x2, waiting for transfers between devices, carried_in(): everything = jax.tree.map(lambda part: lax.all_gather(part, axis), array)  40.3 us
    another operation x2, loops' own time, carried_in(): return lax.fori_loop(0, peers, hop, start)  39.2 us
    select_n x16, other arithmetic, hop(): return jax.tree.map(lambda a, b: jnp.where(reached, a, b), new, before)  23.4 us
    dynamic_slice x32, local copies, waits for them, and re-layouts, hop(): new = combine(before, jax.tree.map(lambda part: part[at], everything))  18.3 us
    unnamed x1, blocking collectives  12.6 us
    unnamed x23, local copies, waits for them, and re-layouts  8.08 us
    ppermute x4, starting transfers between devices, from_partner(): lax.ppermute(array, axis, [(i, i ^ 1 << distance) for i in range(lax.axis...  6.33 us
    ppermute x4, waiting for transfers between devices, from_partner(): lax.ppermute(array, axis, [(i, i ^ 1 << distance) for i in range(lax.axis...  4 us
  transfers between devices with their start and end apart: 6, of which 3 were waited for; matrix products, arithmetic and copies ran while one was open for 37% of the time, Pallas kernels for 0%

commit v1 on v0

v1 whole, which is shorter than its diff:
```python
import functools

import jax
import jax.numpy as jnp
from jax import lax
from jax.experimental import pallas as pl
from jax.experimental.pallas import tpu as pltpu
from jax.sharding import PartitionSpec as P

MESH = pl.DeviceIdType.MESH
BF = jnp.bfloat16
F32 = jnp.float32
NT = (((1,), (1,)), ((), ()))
NN = (((1,), (0,)), ((), ()))
TN = (((0,), (0,)), ((), ()))


def mm(a, b, dims=NN):
    return lax.dot_general(a, b, dims, preferred_element_type=F32)


def split(v):
    hi = v.astype(BF)
    return hi, (v - hi.astype(F32)).astype(BF)


def kernel(
    peers, x_ref, ld_ref, b_ref, c_ref, seg_ref, skip_ref, d_ref,
    ssd_ref, gx_ref, gb_ref, gc_ref,
    bc, info, acum_s, acx, we_s, ws_s, wxh, wxl, wdh, wdl, bias, score_s, dsc,
    ssd_acc, gx_acc, fg, full, half, tbuf, slots, st, gacc, grecv,
    bc_send, bc_recv, i_send, i_recv, d_send, d_recv, t_send, t_recv, s_send, s_recv, g_send, g_recv,
):
    tokens, width = x_ref.shape
    heads = ld_ref.shape[0]
    head = width // heads
    hw = width // 2
    pairs = width // 128
    chips = peers // 2
    me = lax.axis_index("ctx")
    hd = lax.axis_index("head")
    side = hd % 2
    mate = hd + 1 - 2 * side
    core = me % 2
    chip = me // 2
    sib = me + 1 - 2 * core

    barrier = pltpu.get_barrier_semaphore()
    for off in range(1, peers):
        pl.semaphore_signal(barrier, inc=1, device_id={"ctx": (me + off) % peers}, device_id_type=MESH)
    pl.semaphore_signal(barrier, inc=1, device_id={"head": mate}, device_id_type=MESH)

    low = lax.broadcasted_iota(jnp.int32, (1, 128), 1) < head
    rows = lax.broadcasted_iota(jnp.int32, (tokens, tokens), 0)
    cols = lax.broadcasted_iota(jnp.int32, (tokens, tokens), 1)
    ones = jnp.where(rows <= cols, 1.0, 0.0).astype(BF)
    ld = ld_ref[...]
    l0 = ld.astype(BF)
    r1 = ld - l0.astype(F32)
    l1 = r1.astype(BF)
    l2 = (r1 - l1.astype(F32)).astype(BF)
    acum = mm(l0, ones) + mm(l1, ones) + mm(l2, ones)
    acum_s[...] = acum
    acum_t = jnp.concatenate([acum, jnp.zeros((128 - heads, tokens), F32)], axis=0).T
    for p in range(pairs):
        acx[:, p * 128 : (p + 1) * 128] = jnp.where(
            low, acum_t[:, 2 * p : 2 * p + 1], acum_t[:, 2 * p + 1 : 2 * p + 2]
        )
    seg_row = seg_ref[...].astype(F32)
    seg_col = jnp.broadcast_to(seg_row, (128, tokens)).T
    last = jnp.broadcast_to(seg_row[:, tokens - 1 : tokens], (1, hw))
    info[me, 0:1, :] = acx[tokens - 1 : tokens, 0:hw]
    info[me, 1:2, :] = acx[tokens - 1 : tokens, hw:width]
    info[me, 2:3, :] = last
    info[me, 3:4, :] = last

    pl.semaphore_wait(barrier, peers)

    bc_copies = []
    for k, ref in enumerate((b_ref, c_ref)):
        copy = pltpu.make_async_remote_copy(
            src_ref=ref, dst_ref=bc.at[k, side], send_sem=bc_send.at[k], recv_sem=bc_recv.at[k],
            device_id={"head": mate}, device_id_type=MESH)
        copy.start()
        bc_copies.append(copy)
    i_copies = []
    for off in range(1, peers):
        copy = pltpu.make_async_remote_copy(
            src_ref=info.at[me], dst_ref=info.at[me], send_sem=i_send.at[off - 1], recv_sem=i_recv.at[off - 1],
            device_id={"ctx": (me + off) % peers}, device_id_type=MESH)
        copy.start()
        i_copies.append(copy)
    bc[0, side] = b_ref[...]
    bc[1, side] = c_ref[...]

    bias[...] = jnp.where(
        (rows >= cols) & (jnp.concatenate([seg_col] * (tokens // 128), axis=1) == seg_row), 0.0, -1e30
    )
    end_mask = jnp.where(seg_col == last[:, 0:128], 1.0, 0.0)
    for p in range(pairs):
        s = slice(p * 128, (p + 1) * 128)
        a = acx[:, s]
        we = jnp.exp(a[tokens - 1 : tokens, :] - a) * end_mask
        we_s[:, s] = we
        hi, lo = split(x_ref[:, s].astype(F32) * we)
        wxh[:, s] = hi
        wxl[:, s] = lo

    for off in range(1, peers):
        src = (me + peers - off) % peers
        pltpu.make_async_remote_copy(
            src_ref=info.at[src], dst_ref=info.at[src], send_sem=i_send.at[off - 1], recv_sem=i_recv.at[off - 1],
            device_id={"ctx": (me + off) % peers}, device_id_type=MESH).wait_recv()

    def seg_of(i):
        return info[(i + peers) % peers, 2:3, :]

    def prev_seg(i):
        return jnp.where(i == 0, -1.0, seg_of(i - 1))

    start_mask = jnp.where(seg_col == prev_seg(me)[:, 0:128], 1.0, 0.0)
    for p in range(pairs):
        s = slice(p * 128, (p + 1) * 128)
        ws = jnp.exp(acx[:, s]) * start_mask
        ws_s[:, s] = ws
        hi, lo = split(d_ref[:, s].astype(F32) * ws)
        wdh[:, s] = hi
        wdl[:, s] = lo

    for copy in bc_copies:
        copy.wait_recv()
    b_full = jnp.concatenate([bc[0, 0], bc[0, 1]], axis=1)
    c_full = jnp.concatenate([bc[1, 0], bc[1, 1]], axis=1)
    b_t = b_full.T
    c_t = c_full.T
    for k in range(2):
        s = slice(k * hw, (k + 1) * hw)
        fg[0, k] = mm(b_t, wxh[:, s]) + mm(b_t, wxl[:, s])
        fg[1, k] = mm(c_t, wdh[:, s]) + mm(c_t, wdl[:, s])

    half_copy = pltpu.make_async_remote_copy(
        src_ref=fg.at[1 - core, 1 - core], dst_ref=half, send_sem=d_send.at[0], recv_sem=d_recv.at[0],
        device_id={"ctx": sib}, device_id_type=MESH)
    half_copy.start()
    full_copy = pltpu.make_async_remote_copy(
        src_ref=fg.at[core], dst_ref=full, send_sem=d_send.at[1], recv_sem=d_recv.at[1],
        device_id={"ctx": sib}, device_id_type=MESH)
    full_copy.start()

    def carry(i, k):
        return jnp.exp(info[i, pl.ds(k, 1), :]) * jnp.where(seg_of(i) == prev_seg(i), 1.0, 0.0)

    half_copy.wait_recv()
    tbuf[core] = half[...] + carry(sib, core) * fg[core, core]
    full_copy.wait_recv()
    tbuf[1 - core] = fg[1 - core, core] + carry(me, core) * full[core]
    t_copies = []
    for off in range(1, chips):
        copy = pltpu.make_async_remote_copy(
            src_ref=tbuf.at[(chip + off) // chips], dst_ref=slots.at[off - 1],
            send_sem=t_send.at[off - 1], recv_sem=t_recv.at[off - 1],
            device_id={"ctx": ((chip + off) % chips) * 2 + core}, device_id_type=MESH)
        copy.start()
        t_copies.append(copy)

    score_s[...] = mm(c_full, b_full, NT)
    dsc[...] = jnp.zeros_like(dsc)

    def pair_step(p, carried):
        s = pl.ds(pl.multiple_of(p * 128, 128), 128)
        x = x_ref[:, s]
        d = d_ref[:, s]
        gain = jnp.where(low, skip_ref[2 * p], skip_ref[2 * p + 1])
        out = gain * x.astype(F32)
        gx = gain * d.astype(F32)
        zero = jnp.zeros_like(x)
        total = dsc[...]
        for k in range(2):
            mine = low if k == 0 else jnp.logical_not(low)
            xm = jnp.where(mine, x, zero)
            dm = jnp.where(mine, d, zero)
            a_col = acx[:, s][:, k * head : k * head + 1]
            a_row = acum_s[pl.ds(2 * p + k, 1), :]
            table = jnp.exp((a_col - a_row) + bias[...])
            mixed = (table * score_s[...]).astype(BF)
            out = out + mm(mixed, xm)
            gx = gx + mm(mixed, dm, TN)
            total = total + mm(dm, x, NT) * table
        dsc[...] = total
        ssd_acc[:, s] = out
        gx_acc[:, s] = gx
        return carried

    lax.fori_loop(0, pairs, pair_step, 0)

    ds_hi, ds_lo = split(dsc[...])
    gb = mm(ds_hi, c_full, TN) + mm(ds_lo, c_full, TN)
    gc = mm(ds_hi, b_full) + mm(ds_lo, b_full)

    st[core, 0] = jnp.zeros(st.shape[2:], F32)
    st[core, 1] = jnp.zeros(st.shape[2:], F32)
    for off in range(1, chips):
        src = (chip + chips - off) % chips
        later = 1 - (chip + chips - off) // chips
        first = jnp.minimum(src, chip)
        final = jnp.maximum(src, chip)
        total = jnp.zeros((1, hw), F32)
        for i in range(peers):
            within = (i >= 2 * first + 2) & (i < 2 * final)
            total = total + jnp.where(within, info[i, pl.ds(core, 1), :], 0.0)
        weight = jnp.exp(total) * jnp.where(seg_of(2 * first + 1) == seg_of(2 * final - 1), 1.0, 0.0)
        pltpu.make_async_remote_copy(
            src_ref=tbuf.at[0], dst_ref=slots.at[off - 1],
            send_sem=t_send.at[off - 1], recv_sem=t_recv.at[off - 1],
            device_id={"ctx": ((chip + off) % chips) * 2 + core}, device_id_type=MESH).wait_recv()
        st[core, later] = st[core, later] + weight * slots[off - 1]
    s_copy = pltpu.make_async_remote_copy(
        src_ref=st.at[core], dst_ref=st.at[core], send_sem=s_send, recv_sem=s_recv,
        device_id={"ctx": sib}, device_id_type=MESH)
    s_copy.start()
    s_copy.wait_send()
    pltpu.make_async_remote_copy(
        src_ref=st.at[1 - core], dst_ref=st.at[1 - core], send_sem=s_send, recv_sem=s_recv,
        device_id={"ctx": sib}, device_id_type=MESH).wait_recv()
    for k in range(2):
        st[k, 1 - core] = carry(sib, k) * st[k, 1 - core] + full[k]

    for k in range(2):
        s = slice(k * hw, (k + 1) * hw)
        s_hi, s_lo = split(st[k, 0])
        a_hi, a_lo = split(st[k, 1])
        gb = gb + mm(wxh[:, s], a_hi, NT) + mm(wxl[:, s], a_hi, NT) + mm(wxh[:, s], a_lo, NT)
        gc = gc + mm(wdh[:, s], s_hi, NT) + mm(wdl[:, s], s_hi, NT) + mm(wdh[:, s], s_lo, NT)
    n = gb.shape[1] // 2
    for k in range(2):
        gacc[k, 0] = gb[:, k * n : (k + 1) * n]
        gacc[k, 1] = gc[:, k * n : (k + 1) * n]
    g_copy = pltpu.make_async_remote_copy(
        src_ref=gacc.at[1 - side], dst_ref=grecv, send_sem=g_send, recv_sem=g_recv,
        device_id={"head": mate}, device_id_type=MESH)
    g_copy.start()

    for k in range(2):
        s = slice(k * hw, (k + 1) * hw)
        s_hi, s_lo = split(st[k, 0])
        a_hi, a_lo = split(st[k, 1])
        ssd_ref[:, s] = (ssd_acc[:, s] + ws_s[:, s] * (mm(c_full, s_hi) + mm(c_full, s_lo))).astype(BF)
        gx_ref[:, s] = (gx_acc[:, s] + we_s[:, s] * (mm(b_full, a_hi) + mm(b_full, a_lo))).astype(BF)

    g_copy.wait_recv()
    gb_ref[...] = (gacc[side, 0] + grecv[0]).astype(BF)
    gc_ref[...] = (gacc[side, 1] + grecv[1]).astype(BF)

    for copy in bc_copies + i_copies + [half_copy, full_copy] + t_copies + [g_copy]:
        copy.wait_send()


def per_device(peers, inputs, log_decay, in_b, in_c, seg_ids, skip_gain, grad_out):
    tokens, width = inputs.shape
    heads = log_decay.shape[0]
    cols = in_b.shape[1]
    n = 2 * cols
    hw = width // 2
    chips = peers // 2
    vm = pl.BlockSpec(memory_space=pltpu.VMEM)
    dma = pltpu.SemaphoreType.DMA
    return pl.pallas_call(
        functools.partial(kernel, peers),
        out_shape=(
            jax.ShapeDtypeStruct((tokens, width), BF),
            jax.ShapeDtypeStruct((tokens, width), BF),
            jax.ShapeDtypeStruct((tokens, cols), BF),
            jax.ShapeDtypeStruct((tokens, cols), BF),
        ),
        in_specs=[vm, vm, vm, vm, vm, pl.BlockSpec(memory_space=pltpu.SMEM), vm],
        out_specs=(vm, vm, vm, vm),
        scratch_shapes=[
            pltpu.VMEM((2, 2, tokens, cols), BF),
            pltpu.VMEM((peers, 4, hw), F32),
            pltpu.VMEM((heads, tokens), F32),
            pltpu.VMEM((tokens, width), F32),
            pltpu.VMEM((tokens, width), F32),
            pltpu.VMEM((tokens, width), F32),
            pltpu.VMEM((tokens, width), BF),
            pltpu.VMEM((tokens, width), BF),
            pltpu.VMEM((tokens, width), BF),
            pltpu.VMEM((tokens, width), BF),
            pltpu.VMEM((tokens, tokens), F32),
            pltpu.VMEM((tokens, tokens), F32),
            pltpu.VMEM((tokens, tokens), F32),
            pltpu.VMEM((tokens, width), F32),
            pltpu.VMEM((tokens, width), F32),
            pltpu.VMEM((2, 2, n, hw), F32),
            pltpu.VMEM((2, n, hw), F32),
            pltpu.VMEM((n, hw), F32),
            pltpu.VMEM((2, n, hw), F32),
            pltpu.VMEM((chips - 1, n, hw), F32),
            pltpu.VMEM((2, 2, n, hw), F32),
            pltpu.VMEM((2, 2, tokens, cols), F32),
            pltpu.VMEM((2, tokens, cols), F32),
            dma((2,)),
            dma((2,)),
            dma((peers - 1,)),
            dma((peers - 1,)),
            dma((2,)),
            dma((2,)),
            dma((chips - 1,)),
            dma((chips - 1,)),
            dma,
            dma,
            dma,
            dma,
        ],
        compiler_params=pltpu.CompilerParams(
            collective_id=0, has_side_effects=True, vmem_limit_bytes=48 << 20
        ),
    )(inputs, log_decay, in_b, in_c, seg_ids.reshape(1, tokens), skip_gain, grad_out)


def solution(mesh):
    return jax.shard_map(
        functools.partial(per_device, mesh.shape["ctx"]),
        mesh=mesh,
        in_specs=(
            P("ctx", "head"),
            P("head", "ctx"),
            P("ctx", "head"),
            P("ctx", "head"),
            P("ctx"),
            P("head"),
            P("ctx", "head"),
        ),
        out_specs=(P("ctx", "head"), P("ctx", "head"), P("ctx", "head"), P("ctx", "head")),
        check_vma=False,
    )
```

time: 198 us -> 58.1 us (0.29)
  Pallas kernels: 0 us -> 49.1 us
  waiting for transfers between devices: 44.3 us -> 0 us
  loops' own time: 39.2 us -> 0 us
  other arithmetic: 31.4 us -> 0 us
  matrix products: 18.6 us -> 0 us
  local copies, waits for them, and re-layouts: 26.6 us -> 8 us
  between operations: 17.3 us -> 0.66 us
  blocking collectives: 12.6 us -> 0 us
  starting transfers between devices: 6.41 us -> 0 us
    pallas_call x0 -> x1, Pallas kernels: none -> 49.1 us  [per_device(): pl.pallas_call(functools.partial(kernel, peers), out_shape=(jax.ShapeDtyp...]
    all_gather x2 -> x0, waiting for transfers between devices: 40.3 us -> none  [carried_in(): everything = jax.tree.map(lambda part: lax.all_gather(part, axis), array)]
    another operation x2 -> x0, loops' own time: 39.2 us -> none  [carried_in(): return lax.fori_loop(0, peers, hop, start)]
    select_n x18 -> x0, other arithmetic: 24.2 us -> none  [the longest x16 23.4 us: hop(): return jax.tree.map(lambda a, b: jnp.where(reached, a, b), new, before)]
    dot_general x12 -> x0, matrix products: 18.6 us -> none  [the longest x1 2.56 us: local_pass(): jnp.einsum('jn,hpn->jhp', b_block, adjoint, precision=precise, preferred_...]
    dynamic_slice x32 -> x0, local copies, waits for them, and re-layouts: 18.3 us -> none  [hop(): new = combine(before, jax.tree.map(lambda part: part[at], everything))]
    unnamed x1 -> x0, blocking collectives: 12.6 us -> none
    ppermute x4 -> x0, starting transfers between devices: 6.33 us -> none  [from_partner(): lax.ppermute(array, axis, [(i, i ^ 1 << distance) for i in range(lax.axis...]
  transfers between devices with their start and end apart: 6 -> 0, of which waited for: 3 -> 0; matrix products, arithmetic and copies ran while one was open for 37% -> 0% of each run, Pallas kernels for 0% -> 0%
where the time goes in v1:
time: 58.1 us; the launch traced here: 57.8 us
  Pallas kernels  49.1 us (85%)
  local copies, waits for them, and re-layouts  8 us (14%)
  between operations  0.66 us (1%)
    pallas_call x1, Pallas kernels, per_device(): pl.pallas_call(functools.partial(kernel, peers), out_shape=(jax.ShapeDtyp...  49.1 us
    unnamed x18, local copies, waits for them, and re-layouts  8 us

profile of v1, /device:TPU:0, one launch (start us, length us, event | category | flops | bytes accessed | tf_op | source)
XLA Modules:
  0.0 57.8 jit_solution(7078490041344836013)
XLA Ops:
  0.6 0.0 copy-start.6
  0.6 0.0 copy-start.5
  0.7 0.6 %copy-done.6 = f32[16]{0:T(128)S(1)} copy-done((f32[16]{0:T(128)S(1)}, f32[16]{0:T(128)}, u32[]{:S(2)}) %copy-start.6) | copy-done | bytes 88
  1.3 0.0 copy-done.5
  1.3 0.0 copy-start
  1.3 1.0 %copy-done = bf16[256,1024]{1,0:T(8,128)(2,1)S(1)} copy-done((bf16[256,1024]{1,0:T(8,128)(2,1)S(1)}, bf16[256,1024]{1,0:T(8,128)(2,1)}, u32[]{:S(2)}) %copy-start) | copy-done | bytes 524312
  2.4 0.0 copy-start.1
  2.4 1.0 %copy-done.1 = bf16[256,1024]{1,0:T(8,128)(2,1)S(1)} copy-done((bf16[256,1024]{1,0:T(8,128)(2,1)S(1)}, bf16[256,1024]{1,0:T(8,128)(2,1)}, u32[]{:S(2)}) %copy-start.1) | copy-done | bytes 524312
  3.4 0.0 copy-start.2
  3.4 0.8 %copy-done.2 = bf16[256,128]{1,0:T(8,128)(2,1)S(1)} copy-done((bf16[256,128]{1,0:T(8,128)(2,1)S(1)}, bf16[256,128]{1,0:T(8,128)(2,1)}, u32[]{:S(2)}) %copy-start.2) | copy-done | bytes 65560
  4.3 0.0 copy-start.3
  4.3 0.8 %copy-done.3 = bf16[256,128]{1,0:T(8,128)(2,1)S(1)} copy-done((bf16[256,128]{1,0:T(8,128)(2,1)S(1)}, bf16[256,128]{1,0:T(8,128)(2,1)}, u32[]{:S(2)}) %copy-start.3) | copy-done | bytes 65560
  5.1 0.0 copy-start.4
  5.1 0.7 %copy-done.4 = f32[16,256]{1,0:T(8,128)S(1)} copy-done((f32[16,256]{1,0:T(8,128)S(1)}, f32[16,256]{1,0:T(8,128)}, u32[]{:S(2)}) %copy-start.4) | copy-done | bytes 16408
  5.8 49.1 %shard_map.102 = (bf16[256,1024]{1,0:T(8,128)(2,1)S(1)}, bf16[256,1024]{1,0:T(8,128)(2,1)S(1)}, bf16[256,128]{1,0:T(8,128)(2,1)S(1)}, bf16[256,128]{1,0:T(8,128)(2,1)S(1)}) custom-call(bf16[256,1024]{1,0:T(8,128)(2,1)S(1)} %copy-done, f32[16,256]{1,0:T(8,128)S(1)} %copy-done.4, bf16[256,128]{1,0:T(8,128)(2,1)S(1)} %copy-done.2, ...), custom_call_target="tpu_custom_call" | custom-call | tf_op jit(solution)/shard_map/pallas_call | solution.py:267
  54.9 0.8 %copy.15 = bf16[256,1024]{1,0:T(8,128)(2,1)} copy(bf16[256,1024]{1,0:T(8,128)(2,1)S(1)} %get-tuple-element.8) | data formatting | bytes 1048576
  55.7 0.8 %copy.16 = bf16[256,1024]{1,0:T(8,128)(2,1)} copy(bf16[256,1024]{1,0:T(8,128)(2,1)S(1)} %get-tuple-element.9) | data formatting | bytes 1048576
  56.5 0.6 %copy.17 = bf16[256,128]{1,0:T(8,128)(2,1)} copy(bf16[256,128]{1,0:T(8,128)(2,1)S(1)} %get-tuple-element.10) | data formatting | bytes 131072
  57.1 0.6 %copy.18 = bf16[256,128]{1,0:T(8,128)(2,1)} copy(bf16[256,128]{1,0:T(8,128)(2,1)S(1)} %get-tuple-element.11) | data formatting | bytes 131072
Async XLA Ops:
  0.6 0.7 %copy-start.6 = (f32[16]{0:T(128)S(1)}, f32[16]{0:T(128)}, u32[]{:S(2)}) copy-start(f32[16]{0:T(128)} %skip_ref.1) | copy-start | bytes 196
  0.6 0.7 %copy-start.5 = (s32[256]{0:T(256)S(1)}, s32[256]{0:T(256)}, u32[]{:S(2)}) copy-start(s32[256]{0:T(256)} %param.11) | copy-start | bytes 3076
  1.3 1.0 %copy-start = (bf16[256,1024]{1,0:T(8,128)(2,1)S(1)}, bf16[256,1024]{1,0:T(8,128)(2,1)}, u32[]{:S(2)}) copy-start(bf16[256,1024]{1,0:T(8,128)(2,1)} %x_ref.1) | copy-start | bytes 1572868
  2.4 1.0 %copy-start.1 = (bf16[256,1024]{1,0:T(8,128)(2,1)S(1)}, bf16[256,1024]{1,0:T(8,128)(2,1)}, u32[]{:S(2)}) copy-start(bf16[256,1024]{1,0:T(8,128)(2,1)} %d_ref.1) | copy-start | bytes 1572868
  3.4 0.8 %copy-start.2 = (bf16[256,128]{1,0:T(8,128)(2,1)S(1)}, bf16[256,128]{1,0:T(8,128)(2,1)}, u32[]{:S(2)}) copy-start(bf16[256,128]{1,0:T(8,128)(2,1)} %b_ref.1) | copy-start | bytes 196612
  4.3 0.8 %copy-start.3 = (bf16[256,128]{1,0:T(8,128)(2,1)S(1)}, bf16[256,128]{1,0:T(8,128)(2,1)}, u32[]{:S(2)}) copy-start(bf16[256,128]{1,0:T(8,128)(2,1)} %c_ref.1) | copy-start | bytes 196612
  5.1 0.7 %copy-start.4 = (f32[16,256]{1,0:T(8,128)S(1)}, f32[16,256]{1,0:T(8,128)}, u32[]{:S(2)}) copy-start(f32[16,256]{1,0:T(8,128)} %ld_ref.1) | copy-start | bytes 49156

commit v2 on v1

v2 whole, which is shorter than its diff:
```python
import functools

import jax
import jax.numpy as jnp
from jax import lax
from jax.experimental import pallas as pl
from jax.experimental.pallas import tpu as pltpu
from jax.sharding import PartitionSpec as P

MESH = pl.DeviceIdType.MESH
BF = jnp.bfloat16
F32 = jnp.float32
PARTS = 4
VMEM2 = 16 << 20
NT = (((1,), (1,)), ((), ()))
NN = (((1,), (0,)), ((), ()))
TN = (((0,), (0,)), ((), ()))


def mm(a, b, dims=NN):
    return lax.dot_general(a, b, dims, preferred_element_type=F32)


def split(v):
    hi = v.astype(BF)
    return hi, (v - hi.astype(F32)).astype(BF)


def kernel(
    peers, x_hbm, ld_hbm, b_hbm, c_hbm, seg_hbm, skip_hbm, d_hbm,
    ssd_ref, gx_ref, gb_ref, gc_ref,
    x_ref, ld_ref, seg_ref, skip_ref, d_ref, in_sem, bc, info, acum_s, acx, we_s, ws_s, wxh, wxl, wdh, wdl, bias, score_s, dsc,
    ssd_acc, gx_acc, fg, full, half, tbuf, slots, st, gacc, grecv,
    bc_send, bc_recv, i_send, i_recv, d_send, d_recv, t_send, t_recv, s_send, s_recv, g_send, g_recv,
):
    tokens, width = x_hbm.shape
    heads = ld_hbm.shape[0]
    head = width // heads
    hw = width // 2
    pairs = width // 128
    chips = peers // 2
    me = lax.axis_index("ctx")
    hd = lax.axis_index("head")
    side = hd % 2
    mate = hd + 1 - 2 * side
    core = me % 2
    chip = me // 2
    sib = me + 1 - 2 * core

    inputs = [
        pltpu.make_async_copy(src, dst, in_sem.at[k])
        for k, (src, dst) in enumerate((
            (ld_hbm, ld_ref), (seg_hbm, seg_ref), (x_hbm, x_ref), (d_hbm, d_ref), (skip_hbm, skip_ref),
            (b_hbm, bc.at[0, side]), (c_hbm, bc.at[1, side])))
    ]
    for copy in inputs:
        copy.start()

    barrier = pltpu.get_barrier_semaphore()
    for off in range(1, peers):
        pl.semaphore_signal(barrier, inc=1, device_id={"ctx": (me + off) % peers}, device_id_type=MESH)
    pl.semaphore_signal(barrier, inc=1, device_id={"head": mate}, device_id_type=MESH)

    low = lax.broadcasted_iota(jnp.int32, (1, 128), 1) < head
    rows = lax.broadcasted_iota(jnp.int32, (tokens, tokens), 0)
    cols = lax.broadcasted_iota(jnp.int32, (tokens, tokens), 1)
    ones = jnp.where(rows <= cols, 1.0, 0.0).astype(BF)
    inputs[0].wait()
    ld = ld_ref[...]
    l0 = ld.astype(BF)
    r1 = ld - l0.astype(F32)
    l1 = r1.astype(BF)
    l2 = (r1 - l1.astype(F32)).astype(BF)
    acum = mm(l0, ones) + mm(l1, ones) + mm(l2, ones)
    acum_s[...] = acum
    acum_t = jnp.concatenate([acum, jnp.zeros((128 - heads, tokens), F32)], axis=0).T
    for p in range(pairs):
        acx[:, p * 128 : (p + 1) * 128] = jnp.where(
            low, acum_t[:, 2 * p : 2 * p + 1], acum_t[:, 2 * p + 1 : 2 * p + 2]
        )
    inputs[1].wait()
    seg_row = seg_ref[...].astype(F32)
    seg_col = jnp.broadcast_to(seg_row, (128, tokens)).T
    last = jnp.broadcast_to(seg_row[:, tokens - 1 : tokens], (1, hw))
    info[me, 0:1, :] = acx[tokens - 1 : tokens, 0:hw]
    info[me, 1:2, :] = acx[tokens - 1 : tokens, hw:width]
    info[me, 2:3, :] = last
    info[me, 3:4, :] = last

    inputs[2].wait()
    end_mask = jnp.where(seg_col == last[:, 0:128], 1.0, 0.0)
    for p in range(pairs):
        s = slice(p * 128, (p + 1) * 128)
        a = acx[:, s]
        we = jnp.exp(a[tokens - 1 : tokens, :] - a) * end_mask
        we_s[:, s] = we
        hi, lo = split(x_ref[:, s].astype(F32) * we)
        wxh[:, s] = hi
        wxl[:, s] = lo

    pl.semaphore_wait(barrier, peers)

    bc_copies = []
    for k, ref in enumerate((b_hbm, c_hbm)):
        copy = pltpu.make_async_remote_copy(
            src_ref=ref, dst_ref=bc.at[k, side], send_sem=bc_send.at[k], recv_sem=bc_recv.at[k],
            device_id={"head": mate}, device_id_type=MESH)
        copy.start()
        bc_copies.append(copy)
    i_copies = []
    for off in range(1, peers):
        copy = pltpu.make_async_remote_copy(
            src_ref=info.at[me], dst_ref=info.at[me], send_sem=i_send.at[off - 1], recv_sem=i_recv.at[off - 1],
            device_id={"ctx": (me + off) % peers}, device_id_type=MESH)
        copy.start()
        i_copies.append(copy)

    for off in range(1, peers):
        src = (me + peers - off) % peers
        pltpu.make_async_remote_copy(
            src_ref=info.at[src], dst_ref=info.at[src], send_sem=i_send.at[off - 1], recv_sem=i_recv.at[off - 1],
            device_id={"ctx": (me + off) % peers}, device_id_type=MESH).wait_recv()

    def seg_of(i):
        return info[(i + peers) % peers, 2:3, :]

    def prev_seg(i):
        return jnp.where(i == 0, -1.0, seg_of(i - 1))

    inputs[3].wait()
    start_mask = jnp.where(seg_col == prev_seg(me)[:, 0:128], 1.0, 0.0)
    for p in range(pairs):
        s = slice(p * 128, (p + 1) * 128)
        ws = jnp.exp(acx[:, s]) * start_mask
        ws_s[:, s] = ws
        hi, lo = split(d_ref[:, s].astype(F32) * ws)
        wdh[:, s] = hi
        wdl[:, s] = lo

    for copy in bc_copies:
        copy.wait_recv()
    inputs[5].wait()
    inputs[6].wait()
    b_full = jnp.concatenate([bc[0, 0], bc[0, 1]], axis=1)
    c_full = jnp.concatenate([bc[1, 0], bc[1, 1]], axis=1)
    b_t = b_full.T
    c_t = c_full.T
    def carry(i, k):
        return jnp.exp(info[i, pl.ds(k, 1), :]) * jnp.where(seg_of(i) == prev_seg(i), 1.0, 0.0)

    parts = fg.shape[0]
    cw = fg.shape[4]
    d_copies = []
    for q in range(parts):
        for k in range(2):
            s = slice(k * hw + q * cw, k * hw + (q + 1) * cw)
            fg[q, 0, k] = mm(b_t, wxh[:, s]) + mm(b_t, wxl[:, s])
            fg[q, 1, k] = mm(c_t, wdh[:, s]) + mm(c_t, wdl[:, s])
        half_copy = pltpu.make_async_remote_copy(
            src_ref=fg.at[q, 1 - core, 1 - core], dst_ref=half.at[q],
            send_sem=d_send.at[2 * q], recv_sem=d_recv.at[2 * q],
            device_id={"ctx": sib}, device_id_type=MESH)
        half_copy.start()
        full_copy = pltpu.make_async_remote_copy(
            src_ref=fg.at[q, core], dst_ref=full.at[q],
            send_sem=d_send.at[2 * q + 1], recv_sem=d_recv.at[2 * q + 1],
            device_id={"ctx": sib}, device_id_type=MESH)
        full_copy.start()
        d_copies += [half_copy, full_copy]

    sib_carry = carry(sib, core)
    my_carry = carry(me, core)
    t_copies = []
    for q in range(parts):
        u = slice(q * cw, (q + 1) * cw)
        d_copies[2 * q].wait_recv()
        tbuf[q, core] = half[q] + sib_carry[:, u] * fg[q, core, core]
        d_copies[2 * q + 1].wait_recv()
        tbuf[q, 1 - core] = fg[q, 1 - core, core] + my_carry[:, u] * full[q, core]
        for off in range(1, chips):
            at = q * (chips - 1) + off - 1
            copy = pltpu.make_async_remote_copy(
                src_ref=tbuf.at[q, (chip + off) // chips], dst_ref=slots.at[at],
                send_sem=t_send.at[at], recv_sem=t_recv.at[at],
                device_id={"ctx": ((chip + off) % chips) * 2 + core}, device_id_type=MESH)
            copy.start()
            t_copies.append(copy)

    bias[...] = jnp.where(
        (rows >= cols) & (jnp.concatenate([seg_col] * (tokens // 128), axis=1) == seg_row), 0.0, -1e30
    )
    inputs[4].wait()
    score_s[...] = mm(c_full, b_full, NT)
    dsc[...] = jnp.zeros_like(dsc)

    def pair_step(p, carried):
        s = pl.ds(pl.multiple_of(p * 128, 128), 128)
        x = x_ref[:, s]
        d = d_ref[:, s]
        gain = jnp.where(low, skip_ref[2 * p], skip_ref[2 * p + 1])
        out = gain * x.astype(F32)
        gx = gain * d.astype(F32)
        zero = jnp.zeros_like(x)
        total = dsc[...]
        for k in range(2):
            mine = low if k == 0 else jnp.logical_not(low)
            xm = jnp.where(mine, x, zero)
            dm = jnp.where(mine, d, zero)
            a_col = acx[:, s][:, k * head : k * head + 1]
            a_row = acum_s[pl.ds(2 * p + k, 1), :]
            table = jnp.exp((a_col - a_row) + bias[...])
            mixed = (table * score_s[...]).astype(BF)
            out = out + mm(mixed, xm)
            gx = gx + mm(mixed, dm, TN)
            total = total + mm(dm, x, NT) * table
        dsc[...] = total
        ssd_acc[:, s] = out
        gx_acc[:, s] = gx
        return carried

    lax.fori_loop(0, pairs, pair_step, 0)

    ds_hi, ds_lo = split(dsc[...])
    gb = mm(ds_hi, c_full, TN) + mm(ds_lo, c_full, TN)
    gc = mm(ds_hi, b_full) + mm(ds_lo, b_full)

    weights = []
    for off in range(1, chips):
        src = (chip + chips - off) % chips
        first = jnp.minimum(src, chip)
        final = jnp.maximum(src, chip)
        total = jnp.zeros((1, hw), F32)
        for i in range(peers):
            within = (i >= 2 * first + 2) & (i < 2 * final)
            total = total + jnp.where(within, info[i, pl.ds(core, 1), :], 0.0)
        weights.append(jnp.exp(total) * jnp.where(seg_of(2 * first + 1) == seg_of(2 * final - 1), 1.0, 0.0))
    sib_both = [carry(sib, k) for k in range(2)]

    def gather(q):
        u = slice(q * cw, (q + 1) * cw)
        st[q, core, 0] = jnp.zeros(st.shape[3:], F32)
        st[q, core, 1] = jnp.zeros(st.shape[3:], F32)
        for off in range(1, chips):
            later = 1 - (chip + chips - off) // chips
            at = q * (chips - 1) + off - 1
            t_copies[at].wait_recv()
            st[q, core, later] = st[q, core, later] + weights[off - 1][:, u] * slots[at]
        copy = pltpu.make_async_remote_copy(
            src_ref=st.at[q, core], dst_ref=st.at[q, core], send_sem=s_send.at[q], recv_sem=s_recv.at[q],
            device_id={"ctx": sib}, device_id_type=MESH)
        copy.start()
        return copy

    def absorb(q, copy, gb, gc):
        u = slice(q * cw, (q + 1) * cw)
        copy.wait_send()
        pltpu.make_async_remote_copy(
            src_ref=st.at[q, 1 - core], dst_ref=st.at[q, 1 - core], send_sem=s_send.at[q], recv_sem=s_recv.at[q],
            device_id={"ctx": sib}, device_id_type=MESH).wait_recv()
        for k in range(2):
            s = slice(k * hw + q * cw, k * hw + (q + 1) * cw)
            st[q, k, 1 - core] = sib_both[k][:, u] * st[q, k, 1 - core] + full[q, k]
            s_hi, s_lo = split(st[q, k, 0])
            a_hi, a_lo = split(st[q, k, 1])
            gb = gb + mm(wxh[:, s], a_hi, NT) + mm(wxl[:, s], a_hi, NT) + mm(wxh[:, s], a_lo, NT)
            gc = gc + mm(wdh[:, s], s_hi, NT) + mm(wdl[:, s], s_hi, NT) + mm(wdh[:, s], s_lo, NT)
        return gb, gc

    def outputs(q):
        for k in range(2):
            s = slice(k * hw + q * cw, k * hw + (q + 1) * cw)
            s_hi, s_lo = split(st[q, k, 0])
            a_hi, a_lo = split(st[q, k, 1])
            ssd_ref[:, s] = (ssd_acc[:, s] + ws_s[:, s] * (mm(c_full, s_hi) + mm(c_full, s_lo))).astype(BF)
            gx_ref[:, s] = (gx_acc[:, s] + we_s[:, s] * (mm(b_full, a_hi) + mm(b_full, a_lo))).astype(BF)

    s_copy = gather(0)
    for q in range(parts):
        here = s_copy
        if q + 1 < parts:
            gb, gc = absorb(q, here, gb, gc)
            outputs(q)
            s_copy = gather(q + 1)
        else:
            gb, gc = absorb(q, here, gb, gc)
    n = gb.shape[1] // 2
    for k in range(2):
        gacc[k, 0] = gb[:, k * n : (k + 1) * n]
        gacc[k, 1] = gc[:, k * n : (k + 1) * n]
    g_copy = pltpu.make_async_remote_copy(
        src_ref=gacc.at[1 - side], dst_ref=grecv, send_sem=g_send, recv_sem=g_recv,
        device_id={"head": mate}, device_id_type=MESH)
    g_copy.start()

    outputs(parts - 1)

    g_copy.wait_recv()
    gb_ref[...] = (gacc[side, 0] + grecv[0]).astype(BF)
    gc_ref[...] = (gacc[side, 1] + grecv[1]).astype(BF)

    for copy in bc_copies + i_copies + d_copies + t_copies + [g_copy]:
        copy.wait_send()


def per_device(peers, inputs, log_decay, in_b, in_c, seg_ids, skip_gain, grad_out):
    tokens, width = inputs.shape
    heads = log_decay.shape[0]
    cols = in_b.shape[1]
    n = 2 * cols
    hw = width // 2
    chips = peers // 2
    cw = hw // PARTS
    vm = pl.BlockSpec(memory_space=pltpu.VMEM)
    dma = pltpu.SemaphoreType.DMA
    results = pl.pallas_call(
        functools.partial(kernel, peers),
        out_shape=(
            jax.ShapeDtypeStruct((tokens, width), BF),
            jax.ShapeDtypeStruct((tokens, width), BF),
            jax.ShapeDtypeStruct((tokens, cols), BF),
            jax.ShapeDtypeStruct((tokens, cols), BF),
        ),
        in_specs=[pl.BlockSpec(memory_space=pltpu.HBM)] * 7,
        out_specs=(vm, vm, vm, vm),
        scratch_shapes=[
            pltpu.VMEM((tokens, width), BF),
            pltpu.VMEM((heads, tokens), F32),
            pltpu.VMEM((1, tokens), jnp.int32),
            pltpu.SMEM((heads,), F32),
            pltpu.VMEM((tokens, width), BF),
            dma((7,)),
            pltpu.VMEM((2, 2, tokens, cols), BF),
            pltpu.VMEM((peers, 4, hw), F32),
            pltpu.VMEM((heads, tokens), F32),
            pltpu.VMEM((tokens, width), F32),
            pltpu.VMEM((tokens, width), F32),
            pltpu.VMEM((tokens, width), F32),
            pltpu.VMEM((tokens, width), BF),
            pltpu.VMEM((tokens, width), BF),
            pltpu.VMEM((tokens, width), BF),
            pltpu.VMEM((tokens, width), BF),
            pltpu.VMEM((tokens, tokens), F32),
            pltpu.VMEM((tokens, tokens), F32),
            pltpu.VMEM((tokens, tokens), F32),
            pltpu.VMEM((tokens, width), F32),
            pltpu.VMEM((tokens, width), F32),
            pltpu.VMEM((PARTS, 2, 2, n, cw), F32),
            pltpu.VMEM((PARTS, 2, n, cw), F32),
            pltpu.VMEM((PARTS, n, cw), F32),
            pltpu.VMEM((PARTS, 2, n, cw), F32),
            pltpu.VMEM((PARTS * (chips - 1), n, cw), F32),
            pltpu.VMEM((PARTS, 2, 2, n, cw), F32),
            pltpu.VMEM((2, 2, tokens, cols), F32),
            pltpu.VMEM((2, tokens, cols), F32),
            dma((2,)),
            dma((2,)),
            dma((peers - 1,)),
            dma((peers - 1,)),
            dma((2 * PARTS,)),
            dma((2 * PARTS,)),
            dma((PARTS * (chips - 1),)),
            dma((PARTS * (chips - 1),)),
            dma((PARTS,)),
            dma((PARTS,)),
            dma,
            dma,
        ],
        compiler_params=pltpu.CompilerParams(
            collective_id=0, has_side_effects=True, vmem_limit_bytes=48 << 20
        ),
    )(*[pltpu.with_memory_space_constraint(a, pltpu.HBM) for a in (inputs, log_decay, in_b, in_c, seg_ids.reshape(1, tokens), skip_gain, grad_out)])
    hbm = pl.BlockSpec(memory_space=pltpu.HBM)
    return pl.pallas_call(
        hand_over,
        out_shape=tuple(jax.ShapeDtypeStruct(r.shape, r.dtype) for r in results),
        in_specs=[hbm] * 4,
        out_specs=(hbm,) * 4,
        scratch_shapes=[dma((4,))],
        compiler_params=pltpu.CompilerParams(vmem_limit_bytes=VMEM2),
    )(*results)


def hand_over(a, b, c, d, out_a, out_b, out_c, out_d, sem):
    copies = [
        pltpu.make_async_copy(src, dst, sem.at[k])
        for k, (src, dst) in enumerate(((a, out_a), (b, out_b), (c, out_c), (d, out_d)))
    ]
    for copy in copies:
        copy.start()
    for copy in copies:
        copy.wait()


def solution(mesh):
    return jax.shard_map(
        functools.partial(per_device, mesh.shape["ctx"]),
        mesh=mesh,
        in_specs=(
            P("ctx", "head"),
            P("head", "ctx"),
            P("ctx", "head"),
            P("ctx", "head"),
            P("ctx"),
            P("head"),
            P("ctx", "head"),
        ),
        out_specs=(P("ctx", "head"), P("ctx", "head"), P("ctx", "head"), P("ctx", "head")),
        check_vma=False,
    )
```

time: 58.1 us -> 48.3 us (0.83)
  local copies, waits for them, and re-layouts: 8 us -> 0 us
  Pallas kernels: 49.1 us -> 47.4 us
    unnamed x18 -> x0, local copies, waits for them, and re-layouts: 8 us -> none
    pallas_call x1, Pallas kernels: 49.1 us -> 46.4 us  [per_device(): pl.pallas_call(functools.partial(kernel, peers), out_shape=(jax.ShapeDtyp...]
    pallas_call x0 -> x1, Pallas kernels: none -> 1.03 us  [per_device(): pl.pallas_call(hand_over, out_shape=tuple((jax.ShapeDtypeStruct(r.shape,...]
where the time goes in v2:
time: 48.3 us; the launch traced here: 48 us
  Pallas kernels  47.4 us (98%)
  between operations  0.64 us (1%)
    pallas_call x1, Pallas kernels, per_device(): pl.pallas_call(functools.partial(kernel, peers), out_shape=(jax.ShapeDtyp...  46.4 us
    pallas_call x1, Pallas kernels, per_device(): pl.pallas_call(hand_over, out_shape=tuple((jax.ShapeDtypeStruct(r.shape,...  1.03 us

profile of v2, /device:TPU:0, one launch (start us, length us, event | category | flops | bytes accessed | tf_op | source)
XLA Modules:
  0.0 48.0 jit_solution(14933545616216907207)
XLA Ops:
  0.6 46.4 %shard_map.102 = (bf16[256,1024]{1,0:T(8,128)(2,1)S(1)}, bf16[256,1024]{1,0:T(8,128)(2,1)S(1)}, bf16[256,128]{1,0:T(8,128)(2,1)S(1)}, bf16[256,128]{1,0:T(8,128)(2,1)S(1)}) custom-call(bf16[256,1024]{1,0:T(8,128)(2,1)} %x_hbm.1, f32[16,256]{1,0:T(8,128)} %ld_hbm.1, bf16[256,128]{1,0:T(8,128)(2,1)} %b_hbm.1, bf16[256,128]{1,0:T(8,128)(2,1)} %c_hbm.1, ...), custom_call_target="tpu_custom_call" | custom-call | tf_op jit(solution)/shard_map/pallas_call | solution.py:315
  47.0 1.0 %shard_map.103 = (bf16[256,1024]{1,0:T(8,128)(2,1)}, bf16[256,1024]{1,0:T(8,128)(2,1)}, bf16[256,128]{1,0:T(8,128)(2,1)}, bf16[256,128]{1,0:T(8,128)(2,1)}) custom-call(bf16[256,1024]{1,0:T(8,128)(2,1)S(1)} %get-tuple-element.8.a, bf16[256,1024]{1,0:T(8,128)(2,1)S(1)} %get-tuple-element.9.b, bf16[256,128]{1,0:T(8,128)(2,1)S(1)} %get-tuple-element.10.c, ...), custom_call_target="tpu_custom_call" | custom-call | tf_op jit(solution)/shard_map/pallas_call | solution.py:373

commit v3 on v2

--- a/solution.py
+++ b/solution.py
@@ -150,7 +150,26 @@
 
     parts = fg.shape[0]
     cw = fg.shape[4]
+    sib_carry = carry(sib, core)
+    my_carry = carry(me, core)
     d_copies = []
+    t_copies = []
+
+    def forward(q):
+        u = slice(q * cw, (q + 1) * cw)
+        d_copies[2 * q].wait_recv()
+        tbuf[q, core] = half[q] + sib_carry[:, u] * fg[q, core, core]
+        d_copies[2 * q + 1].wait_recv()
+        tbuf[q, 1 - core] = fg[q, 1 - core, core] + my_carry[:, u] * full[q, core]
+        for off in range(1, chips):
+            at = q * (chips - 1) + off - 1
+            copy = pltpu.make_async_remote_copy(
+                src_ref=tbuf.at[q, (chip + off) // chips], dst_ref=slots.at[at],
+                send_sem=t_send.at[at], recv_sem=t_recv.at[at],
+                device_id={"ctx": ((chip + off) % chips) * 2 + core}, device_id_type=MESH)
+            copy.start()
+            t_copies.append(copy)
+
     for q in range(parts):
         for k in range(2):
             s = slice(k * hw + q * cw, k * hw + (q + 1) * cw)
@@ -167,24 +186,10 @@
             device_id={"ctx": sib}, device_id_type=MESH)
         full_copy.start()
         d_copies += [half_copy, full_copy]
-
-    sib_carry = carry(sib, core)
-    my_carry = carry(me, core)
-    t_copies = []
-    for q in range(parts):
-        u = slice(q * cw, (q + 1) * cw)
-        d_copies[2 * q].wait_recv()
-        tbuf[q, core] = half[q] + sib_carry[:, u] * fg[q, core, core]
-        d_copies[2 * q + 1].wait_recv()
-        tbuf[q, 1 - core] = fg[q, 1 - core, core] + my_carry[:, u] * full[q, core]
-        for off in range(1, chips):
-            at = q * (chips - 1) + off - 1
-            copy = pltpu.make_async_remote_copy(
-                src_ref=tbuf.at[q, (chip + off) // chips], dst_ref=slots.at[at],
-                send_sem=t_send.at[at], recv_sem=t_recv.at[at],
-                device_id={"ctx": ((chip + off) % chips) * 2 + core}, device_id_type=MESH)
-            copy.start()
-            t_copies.append(copy)
+        if q:
+            forward(q - 1)
+    forward(parts - 1)
+
 
     bias[...] = jnp.where(
         (rows >= cols) & (jnp.concatenate([seg_col] * (tokens // 128), axis=1) == seg_row), 0.0, -1e30
@@ -251,6 +256,19 @@
         copy.start()
         return copy
 
+    n = b_full.shape[1] // 2
+    g_copies = []
+
+    def send_off(which, grad):
+        for k in range(2):
+            gacc[k, which] = grad[:, k * n : (k + 1) * n]
+        g_copy = pltpu.make_async_remote_copy(
+            src_ref=gacc.at[1 - side, which], dst_ref=grecv.at[which],
+            send_sem=g_send.at[which], recv_sem=g_recv.at[which],
+            device_id={"head": mate}, device_id_type=MESH)
+        g_copy.start()
+        g_copies.append(g_copy)
+
     def absorb(q, copy, gb, gc):
         u = slice(q * cw, (q + 1) * cw)
         copy.wait_send()
@@ -260,10 +278,16 @@
         for k in range(2):
             s = slice(k * hw + q * cw, k * hw + (q + 1) * cw)
             st[q, k, 1 - core] = sib_both[k][:, u] * st[q, k, 1 - core] + full[q, k]
-            s_hi, s_lo = split(st[q, k, 0])
             a_hi, a_lo = split(st[q, k, 1])
             gb = gb + mm(wxh[:, s], a_hi, NT) + mm(wxl[:, s], a_hi, NT) + mm(wxh[:, s], a_lo, NT)
+        if q == parts - 1:
+            send_off(0, gb)
+        for k in range(2):
+            s = slice(k * hw + q * cw, k * hw + (q + 1) * cw)
+            s_hi, s_lo = split(st[q, k, 0])
             gc = gc + mm(wdh[:, s], s_hi, NT) + mm(wdl[:, s], s_hi, NT) + mm(wdh[:, s], s_lo, NT)
+        if q == parts - 1:
+            send_off(1, gc)
         return gb, gc
 
     def outputs(q):
@@ -283,22 +307,14 @@
             s_copy = gather(q + 1)
         else:
             gb, gc = absorb(q, here, gb, gc)
-    n = gb.shape[1] // 2
-    for k in range(2):
-        gacc[k, 0] = gb[:, k * n : (k + 1) * n]
-        gacc[k, 1] = gc[:, k * n : (k + 1) * n]
-    g_copy = pltpu.make_async_remote_copy(
-        src_ref=gacc.at[1 - side], dst_ref=grecv, send_sem=g_send, recv_sem=g_recv,
-        device_id={"head": mate}, device_id_type=MESH)
-    g_copy.start()
-
     outputs(parts - 1)
 
-    g_copy.wait_recv()
+    g_copies[0].wait_recv()
     gb_ref[...] = (gacc[side, 0] + grecv[0]).astype(BF)
+    g_copies[1].wait_recv()
     gc_ref[...] = (gacc[side, 1] + grecv[1]).astype(BF)
 
-    for copy in bc_copies + i_copies + d_copies + t_copies + [g_copy]:
+    for copy in bc_copies + i_copies + d_copies + t_copies + g_copies:
         copy.wait_send()
 
 
@@ -362,8 +378,8 @@
             dma((PARTS * (chips - 1),)),
             dma((PARTS,)),
             dma((PARTS,)),
-            dma,
-            dma,
+            dma((2,)),
+            dma((2,)),
         ],
         compiler_params=pltpu.CompilerParams(
             collective_id=0, has_side_effects=True, vmem_limit_bytes=48 << 20

time: 48.3 us -> 48.2 us (level)
  no operation moved by 1% of the time
where the time goes in v3:
time: 48.2 us; the launch traced here: 47.9 us
  Pallas kernels  47.3 us (98%)
  between operations  0.64 us (1%)
    pallas_call x1, Pallas kernels, per_device(): pl.pallas_call(functools.partial(kernel, peers), out_shape=(jax.ShapeDtyp...  46.3 us
    pallas_call x1, Pallas kernels, per_device(): pl.pallas_call(hand_over, out_shape=tuple((jax.ShapeDtypeStruct(r.shape,...  1.03 us

profile of v3, /device:TPU:0, one launch (start us, length us, event | category | flops | bytes accessed | tf_op | source)
XLA Modules:
  0.0 47.9 jit_solution(4460371041875615079)
XLA Ops:
  0.6 46.3 %shard_map.102 = (bf16[256,1024]{1,0:T(8,128)(2,1)S(1)}, bf16[256,1024]{1,0:T(8,128)(2,1)S(1)}, bf16[256,128]{1,0:T(8,128)(2,1)S(1)}, bf16[256,128]{1,0:T(8,128)(2,1)S(1)}) custom-call(bf16[256,1024]{1,0:T(8,128)(2,1)} %x_hbm.1, f32[16,256]{1,0:T(8,128)} %ld_hbm.1, bf16[256,128]{1,0:T(8,128)(2,1)} %b_hbm.1, bf16[256,128]{1,0:T(8,128)(2,1)} %c_hbm.1, ...), custom_call_target="tpu_custom_call" | custom-call | tf_op jit(solution)/shard_map/pallas_call | solution.py:331
  46.9 1.0 %shard_map.103 = (bf16[256,1024]{1,0:T(8,128)(2,1)}, bf16[256,1024]{1,0:T(8,128)(2,1)}, bf16[256,128]{1,0:T(8,128)(2,1)}, bf16[256,128]{1,0:T(8,128)(2,1)}) custom-call(bf16[256,1024]{1,0:T(8,128)(2,1)S(1)} %get-tuple-element.8.a, bf16[256,1024]{1,0:T(8,128)(2,1)S(1)} %get-tuple-element.9.b, bf16[256,128]{1,0:T(8,128)(2,1)S(1)} %get-tuple-element.10.c, ...), custom_call_target="tpu_custom_call" | custom-call | tf_op jit(solution)/shard_map/pallas_call | solution.py:389

commit v4 on v3

--- a/solution.py
+++ b/solution.py
@@ -303,8 +303,8 @@
         here = s_copy
         if q + 1 < parts:
             gb, gc = absorb(q, here, gb, gc)
+            s_copy = gather(q + 1)
             outputs(q)
-            s_copy = gather(q + 1)
         else:
             gb, gc = absorb(q, here, gb, gc)
     outputs(parts - 1)

time: 48.2 us -> 48.2 us (level)
  no operation moved by 1% of the time
where the time goes in v4:
time: 48.2 us; the launch traced here: 47.9 us
  Pallas kernels  47.3 us (98%)
  between operations  0.64 us (1%)
    pallas_call x1, Pallas kernels, per_device(): pl.pallas_call(functools.partial(kernel, peers), out_shape=(jax.ShapeDtyp...  46.3 us
    pallas_call x1, Pallas kernels, per_device(): pl.pallas_call(hand_over, out_shape=tuple((jax.ShapeDtypeStruct(r.shape,...  1.03 us

profile of v4, /device:TPU:0, one launch (start us, length us, event | category | flops | bytes accessed | tf_op | source)
XLA Modules:
  0.0 47.9 jit_solution(11162996443512904124)
XLA Ops:
  0.6 46.3 %shard_map.102 = (bf16[256,1024]{1,0:T(8,128)(2,1)S(1)}, bf16[256,1024]{1,0:T(8,128)(2,1)S(1)}, bf16[256,128]{1,0:T(8,128)(2,1)S(1)}, bf16[256,128]{1,0:T(8,128)(2,1)S(1)}) custom-call(bf16[256,1024]{1,0:T(8,128)(2,1)} %x_hbm.1, f32[16,256]{1,0:T(8,128)} %ld_hbm.1, bf16[256,128]{1,0:T(8,128)(2,1)} %b_hbm.1, bf16[256,128]{1,0:T(8,128)(2,1)} %c_hbm.1, ...), custom_call_target="tpu_custom_call" | custom-call | tf_op jit(solution)/shard_map/pallas_call | solution.py:331
  46.9 1.0 %shard_map.103 = (bf16[256,1024]{1,0:T(8,128)(2,1)}, bf16[256,1024]{1,0:T(8,128)(2,1)}, bf16[256,128]{1,0:T(8,128)(2,1)}, bf16[256,128]{1,0:T(8,128)(2,1)}) custom-call(bf16[256,1024]{1,0:T(8,128)(2,1)S(1)} %get-tuple-element.8.a, bf16[256,1024]{1,0:T(8,128)(2,1)S(1)} %get-tuple-element.9.b, bf16[256,128]{1,0:T(8,128)(2,1)S(1)} %get-tuple-element.10.c, ...), custom_call_target="tpu_custom_call" | custom-call | tf_op jit(solution)/shard_map/pallas_call | solution.py:389
